TPU v7x, 32 devices: a whole 2x2x4 slice. The times are simulated.
32 devices in a mesh: dp: 4 (over y, x), shard: 8 (over z, core).
Axes of the slice: x: 2, y: 2, z: 4, core: 2. Of those that a mesh axis runs over, the one named last changes fastest.
Arguments:
- id_table: float32 [262144, 128], P(('dp', 'shard')), may hold values from -6 to 6
- ada_state: float32 [262144], P(('dp', 'shard')), may hold values from 0.01 to 1
- user_first: float32 [128, 512], replicated, may hold values from -0.5 to 0.5
- user_second: float32 [512, 128], replicated, may hold values from -0.25 to 0.25
- item_first: float32 [128, 512], replicated, may hold values from -0.5 to 0.5
- item_second: float32 [512, 128], replicated, may hold values from -0.25 to 0.25
- fetch_rows: int32 [32, 4, 8, 72], P(('dp', 'shard')), may hold values from 0 to 8191
- lookup_slots: int32 [32, 1536], P(('dp', 'shard')), may hold values from 0 to 2303
Outputs:
- new_table: float32 [262144, 128], P(('dp', 'shard'))
- new_state: float32 [262144], P(('dp', 'shard'))
- user_first_grad: float32 [128, 512], replicated
- user_second_grad: float32 [512, 128], replicated
- item_first_grad: float32 [128, 512], replicated
- item_second_grad: float32 [512, 128], replicated
- mean_loss: float32 [], replicated
All inputs are finite; a program needn't handle non-finite values.
Results may differ from a plain program's by a relative error of at most 0.0038.
The roundings to bfloat16 on the way count: a program that leaves them out, or rounds other values in their place, can miss the bound.
Values may be sent and summed in bfloat16 or wider, within the bound.
No kernel may reach another device: no remote copies, remote signals or barrier semaphores. Data moves between devices by JAX's collectives and lax.ppermute only.
A program may use at most 128 MiB of HBM per device.

v0:
```python
import jax
import jax.numpy as jnp
from jax import lax
from jax.sharding import PartitionSpec as P

EXAMPLES_ON_CHIP = 512
highest = lax.Precision.HIGHEST
logit_divisor = 0.025
learn_rate = 0.1
epsilon = 1e-08


def tower_pass(looked, first_w, second_w):
    hidden_act = jax.nn.silu(
        jnp.dot(looked, first_w, precision=highest, preferred_element_type=jnp.float32)
    )
    tower_out = jnp.dot(hidden_act, second_w, precision=highest, preferred_element_type=jnp.float32)
    return tower_out / jnp.sqrt(jnp.sum(tower_out * tower_out, axis=1, keepdims=True) + 1e-06)


def score_block(user_half_precision, candidate_half_precision):
    return (
        jnp.dot(user_half_precision, candidate_half_precision.T, preferred_element_type=jnp.float32)
        / logit_divisor
    )


def cand_step(candidate_half_precision, user_half_precision):
    exponent = jnp.exp(score_block(user_half_precision, candidate_half_precision))
    collected_entries = jnp.dot(
        exponent.astype(jnp.bfloat16), candidate_half_precision, preferred_element_type=jnp.float32
    )
    return (jnp.sum(exponent, axis=1), collected_entries)


def item_term(user_half_precision, log_z, candidate_half_precision):
    softmax = jnp.exp(
        score_block(user_half_precision, candidate_half_precision) - log_z[:, None]
    ).astype(jnp.bfloat16)
    return jnp.dot(softmax.T, user_half_precision, preferred_element_type=jnp.float32)


def per_device(
    id_table, ada_state, user_first, user_second, item_first, item_second, fetch_rows, lookup_slots
):
    target_index_vector = id_table.shape[1]
    examples_on_chip = EXAMPLES_ON_CHIP
    asked_rows = lax.all_to_all(
        lax.all_to_all(fetch_rows[0], "dp", split_axis=0, concat_axis=0, tiled=True),
        "shard",
        split_axis=1,
        concat_axis=1,
        tiled=True,
    )
    fetched = jnp.take(id_table, asked_rows.reshape(-1), axis=0).reshape(
        asked_rows.shape + (target_index_vector,)
    )
    returned = lax.all_to_all(
        lax.all_to_all(fetched, "dp", split_axis=0, concat_axis=0, tiled=True),
        "shard",
        split_axis=1,
        concat_axis=1,
        tiled=True,
    )
    slot_rows = returned.reshape(-1, target_index_vector)
    slot_index = lookup_slots[0]
    looked = jnp.take(slot_rows, slot_index, axis=0)
    user_vec, user_pull = jax.vjp(tower_pass, looked[:examples_on_chip], user_first, user_second)
    item_vec, item_pull = jax.vjp(tower_pass, looked[examples_on_chip:], item_first, item_second)
    user_half_precision = user_vec.astype(jnp.bfloat16)
    item_bf = item_vec.astype(jnp.bfloat16)
    query_single_float = user_half_precision.astype(jnp.float32)
    resident_target_entries = item_bf[:examples_on_chip].astype(jnp.float32)
    matching_pair_logit = (
        jnp.sum(query_single_float * resident_target_entries, axis=1) / logit_divisor
    )
    reduced_aggregates, collected_entries = cand_step(
        lax.all_gather(item_bf, "dp", axis=0, tiled=True), user_half_precision
    )
    log_z = jnp.log(reduced_aggregates)
    target_derivative_accrual = item_term(
        lax.all_gather(user_vec, "dp", axis=0, tiled=True).astype(jnp.bfloat16),
        lax.all_gather(log_z, "dp", axis=0, tiled=True),
        item_bf,
    )
    query_adjoint = (
        collected_entries / reduced_aggregates[:, None] - resident_target_entries
    ) / logit_divisor
    target_adjoint = (
        target_derivative_accrual.at[:examples_on_chip].add(-query_single_float) / logit_divisor
    )
    user_look, user_first_g, user_second_g = user_pull(query_adjoint)
    item_look, item_first_g, item_second_g = item_pull(target_adjoint)
    look_grads = jnp.concatenate([user_look, item_look], axis=0)
    slot_grads = jnp.zeros_like(slot_rows).at[slot_index].add(look_grads)
    sent_back = lax.all_to_all(
        lax.all_to_all(
            slot_grads.reshape(returned.shape).astype(jnp.bfloat16),
            "dp",
            split_axis=0,
            concat_axis=0,
            tiled=True,
        ),
        "shard",
        split_axis=1,
        concat_axis=1,
        tiled=True,
    ).astype(jnp.float32)
    grad_rows = (
        jnp.zeros_like(id_table)
        .at[asked_rows.reshape(-1)]
        .add(sent_back.reshape(-1, target_index_vector))
    )
    new_state = ada_state + jnp.mean(grad_rows * grad_rows, axis=1)
    new_table = id_table - learn_rate * grad_rows / (jnp.sqrt(new_state)[:, None] + epsilon)
    loss_part = jnp.sum(log_z - matching_pair_logit)
    summed = lax.psum(
        (user_first_g, user_second_g, item_first_g, item_second_g, loss_part), ("dp", "shard")
    )
    shard_number = lax.axis_size("dp") * lax.axis_size("shard")
    return (
        new_table,
        new_state,
        summed[0] / shard_number,
        summed[1] / shard_number,
        summed[2] / shard_number,
        summed[3] / shard_number,
        summed[4] / (shard_number * examples_on_chip),
    )


def solution(mesh):
    return jax.shard_map(
        per_device,
        mesh=mesh,
        in_specs=(
            P(("dp", "shard"), None),
            P(("dp", "shard")),
            P(),
            P(),
            P(),
            P(),
            P(("dp", "shard"), None, None, None),
            P(("dp", "shard"), None),
        ),
        out_specs=(P(("dp", "shard"), None), P(("dp", "shard")), P(), P(), P(), P(), P()),
        check_vma=False,
    )
```

profile of v0, /device:TPU:0, one launch (start us, length us, event | category | flops | bytes accessed | tf_op | source)
XLA Modules:
  0.0 361.9 jit_solution(15782953325688524731)
XLA Ops:
  7.2 0.0 copy-start
  7.2 10.0 %all_to_all.30 = s32[4,8,72]{2,1,0:T(8,128)S(1)} all-to-all(s32[4,8,72]{2,1,0:T(8,128)} %bitcast.34), channel_id=1, replica_groups=mesh['dp'=4,'shard'=8] {'dp'}, dimensions={0} | all-to-all | bytes 18432 | tf_op jit(solution)/shard_map/all_to_all | solution.py:49
  17.2 10.3 %all_to_all.31 = s32[4,8,72]{2,0,1:T(4,128)S(1)} all-to-all(s32[4,8,72]{2,0,1:T(4,128)S(1)} %copy.24), channel_id=1, replica_groups=mesh['dp'=4,'shard'=8] {'shard'}, dimensions={1} | all-to-all | bytes 18432 | tf_op jit(solution)/shard_map/all_to_all | solution.py:48
  27.6 0.1 reshape.171
  27.7 0.6 copy-done.14
  28.3 6.1 %gather_fusion = f32[2304,128]{1,0:T(8,128)S(1)} fusion(f32[8192,128]{1,0:T(8,128)} %param.10, s32[3072]{0:T(1024)S(1)} %pad_clamp_fusion), kind=kCustom, calls=%fused_computation | custom fusion | bytes 2368512 | tf_op jit(solution)/shard_map/jit(_take)/gather | solution.py:55
  34.4 0.5 broadcast_select_fusion
  34.9 18.2 %all_to_all.32 = f32[4,8,72,128]{3,2,1,0:T(8,128)S(1)} all-to-all(f32[4,8,72,128]{3,2,1,0:T(8,128)S(1)} %broadcast_select_fusion), channel_id=1, replica_groups=mesh['dp'=4,'shard'=8] {'dp'}, dimensions={0} | all-to-all | bytes 2359296 | tf_op jit(solution)/shard_map/all_to_all | solution.py:59
  53.1 1.1 copy.27
  54.2 3.6 all-to-all-start.3
  57.8 0.0 all-gather.3.cloned.1.call-start
  57.9 29.1 %all-to-all-done.3 = f32[4,8,72,128]{3,2,0,1:T(8,128)S(1)} async-done(((f32[4,8,72,128]{3,2,0,1:T(8,128)}), f32[4,8,72,128]{3,2,0,1:T(8,128)S(1)}, u32[]{:S(2)}, u32[]{:S(2)}) %all-to-all-start.3) | async-done | bytes 1179680 | tf_op jit(solution)/shard_map/all_to_all | solution.py:58
  87.1 0.1 copy.28
  87.2 0.0 copy-start.12
  87.2 2.6 gather_fusion.1
  89.8 0.3 broadcast_select_fusion.1
  90.1 1.8 fusion.30
  91.9 2.7 multiply_reduce_fusion.2
  94.7 0.7 divide_multiply_fusion
  95.4 0.1 copy-done.5
  95.5 0.8 divide_convert_fusion
  96.2 0.0 all-gather.3.cloned.1.call-update
  96.2 1.0 fusion.41
  97.2 0.0 copy-start.3
  97.3 2.7 multiply_reduce_fusion.4
  100.0 0.5 copy-done.23
  100.5 0.1 copy-done.6
  100.7 0.6 fusion.38
  101.3 11.5 %all_gather.10 = bf16[2048,128]{0,1:T(8,128)(2,1)} all-gather(bf16[512,128]{0,1:T(8,128)(2,1)S(1)} %get-tuple-element.24), channel_id=1, replica_groups=mesh['dp'=4,'shard'=8] {'dp'}, dimensions={0}, use_global_device_ids=true | all-gather | bytes 655360 | tf_op jit(solution)/shard_map/all_gather | solution.py:82
  112.8 8.4 %all-gather.3.cloned.1.call-done = bf16[4096,128]{0,1:T(8,128)(2,1)} async-done(((bf16[1024,128]{0,1:T(8,128)(2,1)}), bf16[4096,128]{0,1:T(8,128)(2,1)}) %all-gather.3.cloned.1.call-update) | async-done | bytes 1048592 | tf_op jit(solution)/shard_map/all_gather | solution.py:78
  121.2 5.8 %fusion = (f32[512]{0:T(512)S(1)}, f32[512,4096]{1,0:T(8,128)}) fusion(bf16[512,128]{0,1:T(8,128)(2,1)S(1)} %get-tuple-element.24, bf16[4096,128]{0,1:T(8,128)(2,1)} %all-gather.3.cloned.1.call-done), kind=kOutput, calls=%fused_computation.6 | convolution fusion | flops 541064704 | bytes 9570304 | tf_op jit(solution)/shard_map/dot_general | solution.py:23
  127.0 0.6 subtract_reduce_fusion
  127.6 8.8 %all-gather = f32[4,1,512]{2,1,0:T(1,128)} all-gather(f32[1,1,512]{2,1,0:T(1,128)S(1)} %bitcast.36), channel_id=1, replica_groups=mesh['dp'=4,'shard'=8] {'dp'}, dimensions={0}, use_global_device_ids=true | all-gather | bytes 10240 | tf_op jit(solution)/shard_map/all_gather | solution.py:83
  136.5 4.1 %fusion.10 = f32[1024,128]{0,1:T(8,128)} fusion(bf16[1024,128]{0,1:T(8,128)(2,1)S(1)} %copy-done.3, f32[2048]{0:T(1024)} %bitcast.35, bf16[2048,128]{0,1:T(8,128)(2,1)} %all_gather.10), kind=kOutput, calls=%fused_computation.19 | convolution fusion | flops 1080033280 | bytes 1318912 | tf_op jit(solution)/shard_map/dot_general | solution.py:40
  140.6 1.7 fusion.37
  142.3 1.4 multiply_reduce_fusion.1
  143.7 0.8 multiply_multiply_fusion
  144.6 3.8 %fusion.6 = f32[1024,512]{1,0:T(8,128)S(1)} fusion(f32[1024,512]{1,0:T(8,128)S(1)} %fusion.30, f32[512,128]{1,0:T(8,128)S(1)} %copy-done, f32[1024,128]{0,1:T(8,128)} %copy-done.5, f32[1024,128]{0,1:T(8,128)} %fusion.37, f32[1024]{0:T(1024)S(1)} %multiply_multiply_fusion, f32[1024]{0:T(1024)} %copy-done.17), kind=kOutput, calls=%fused_computation.14 | convolution fusion | flops 810680320 | bytes 5513216 | tf_op jit(solution)/shard_map/transpose(jvp())/dot_general | solution.py:17
  148.4 0.0 copy-start.13
  148.4 2.1 fusion.28
  150.5 2.6 fusion.58
  153.1 1.6 multiply_reduce_fusion.3
  154.8 0.0 copy-start.27
  154.8 2.6 fusion.43
  157.4 1.6 fusion.19
  159.0 1.0 fusion.57
  160.0 9.3 %scatter_custom_fusion = f32[2304,128]{1,0:T(8,128)S(1)} fusion(s32[1536]{0:T(1024)S(1)} %fusion.48, f32[1024,128]{1,0:T(8,128)} %fusion.58, f32[]{:T(128)} %constant.111, f32[512,128]{1,0:T(8,128)S(1)} %fusion.57, f32[]{:T(128)} %constant.90.clone.1), kind=kCustom, calls=%fused_computation.28 | custom fusion | flops 393216 | bytes 1966088 | tf_op jit(solution)/shard_map/scatter-add | solution.py:95
  169.4 0.9 convert_element_type.35
  170.2 3.5 all-to-all-start.4
  173.7 6.2 %fusion.32 = f32[512,128]{1,0:T(8,128)} fusion(f32[1024,512]{1,0:T(8,128)} %copy-done.4, f32[1024,128]{0,1:T(8,128)} %copy-done.5, f32[1024,128]{0,1:T(8,128)} %fusion.37, f32[1024]{0:T(1024)S(1)} %copy-done.26, f32[1024]{0:T(1024)S(1)} %copy-done.18), kind=kOutput, calls=%fused_computation.45 | convolution fusion | flops 808058880 | bytes 3416064 | tf_op jit(solution)/shard_map/transpose(jvp())/dot_general | solution.py:17
  179.9 0.7 all-to-all-done.4
  180.7 0.9 copy.29
  181.5 4.6 %all-to-all-start.5 = ((bf16[4,8,72,128]{3,2,0,1:T(8,128)(2,1)}), bf16[4,8,72,128]{3,2,0,1:T(8,128)(2,1)S(1)}, u32[]{:S(2)}, u32[]{:S(2)}) async-start(bf16[4,8,72,128]{3,2,0,1:T(8,128)(2,1)} %copy.29), calls=%async_computation.5 | async-start | bytes 1179648 | tf_op jit(solution)/shard_map/all_to_all | solution.py:96
  186.1 0.0 all-reduce.3.cloned.1.call-start
  186.2 1.5 fusion.39
  187.6 0.0 all-reduce.3.cloned.1.call-update
  187.7 40.8 %psum.39 = f32[]{:T(128)} all-reduce(f32[]{:T(128)} %get-tuple-element.29), channel_id=1, replica_groups=mesh['dp'=4,'shard'=8] {'dp','shard'}, use_global_device_ids=true, to_apply=%region_14.15 | all-reduce | flops 1 | bytes 8 | tf_op jit(solution)/shard_map/psum | solution.py:117
  229.1 96.8 %all-reduce.3.cloned.1.call-done = (f32[128,512]{1,0:T(8,128)}, f32[512,128]{1,0:T(8,128)}, f32[128,512]{1,0:T(8,128)}, f32[512,128]{1,0:T(8,128)}) async-done(((f32[128,512]{1,0:T(8,128)}, f32[512,128]{1,0:T(8,128)}, f32[128,512]{1,0:T(8,128)}, f32[512,128]{1,0:T(8,128)}), (f32[128,512]{1,0:T(8,128)}, f32[512,128]{1,0:T(8,128)}, f32[128,512]{1,0:T(8,128)}, ...) | async-done | bytes 1048592 | tf_op jit(solution)/shard_map/psum | solution.py:117
  326.0 1.9 broadcast_multiply_fusion.2
  327.8 1.9 broadcast_multiply_fusion
  329.8 15.8 %scatter_custom_fusion.1 = f32[8192,128]{1,0:T(8,128)} fusion(s32[2304]{0:T(1024)} %copy-done.14, f32[]{:T(128)} %constant.90.clone.1, bf16[2304,128]{1,0:T(8,128)(2,1)S(1)} %bitcast.32), kind=kCustom, calls=%fused_computation.17 | custom fusion | flops 589824 | bytes 4784640 | tf_op jit(solution)/shard_map/scatter-add | solution.py:112
  345.6 3.5 multiply_reduce_fusion
  349.1 0.6 sqrt_add_fusion
  349.7 4.2 %divide_subtract_fusion = f32[8192,128]{1,0:T(8,128)} fusion(f32[8192,128]{1,0:T(8,128)S(1)} %copy-done.1, f32[8192,128]{1,0:T(8,128)} %scatter_custom_fusion.1, f32[8192]{0:T(1024)S(1)} %get-tuple-element.25), kind=kLoop, calls=%fused_computation.9 | loop fusion | flops 3145728 | bytes 12615680 | tf_op jit(solution)/shard_map/sub | solution.py:115
  (66 shorter events, 0.3 us)
Async XLA Ops:
  7.2 84.7 %copy-start = (f32[512,128]{1,0:T(8,128)S(1)}, f32[512,128]{1,0:T(8,128)}, u32[]{:S(2)}) copy-start(f32[512,128]{1,0:T(8,128)} %param.15) | copy-start | bytes 786436
  27.7 0.6 copy-start.14
  53.1 4.7 %copy-start.16 = (s32[1,1536]{1,0:T(1,128)S(1)}, s32[1,1536]{1,0:T(1,128)}, u32[]{:S(2)}) copy-start(s32[1,1536]{1,0:T(1,128)} %param.17) | copy-start | bytes 18436
  54.2 32.9 %all-to-all-start.3 = ((f32[4,8,72,128]{3,2,0,1:T(8,128)}), f32[4,8,72,128]{3,2,0,1:T(8,128)S(1)}, u32[]{:S(2)}, u32[]{:S(2)}) async-start(f32[4,8,72,128]{3,2,0,1:T(8,128)} %copy.27), calls=%async_computation.3 | async-start | bytes 2359296 | tf_op jit(solution)/shard_map/all_to_all | solution.py:58
  57.8 63.4 %all-gather.3.cloned.1.call-start = ((), (), s32[]{:S(2)}) async-start(), calls=%async_computation.6 | async-start | bytes 1310720 | tf_op jit(solution)/shard_map/all_gather | solution.py:78
  87.2 2.9 copy-start.12
  91.9 52.7 %copy-start.4 = (f32[1024,512]{1,0:T(8,128)}, f32[1024,512]{1,0:T(8,128)S(1)}, u32[]{:S(2)}) copy-start(f32[1024,512]{1,0:T(8,128)S(1)} %fusion.30) | copy-start | bytes 6291460
  91.9 4.3 %copy-start.10 = (f32[128,512]{1,0:T(8,128)S(1)}, f32[128,512]{1,0:T(8,128)}, u32[]{:S(2)}) copy-start(f32[128,512]{1,0:T(8,128)} %param.12) | copy-start | bytes 786436
  94.7 0.8 copy-start.5
  94.7 5.3 %copy-start.19 = (f32[1024]{0:T(1024)}, f32[1024]{0:T(1024)S(1)}, u32[]{:S(2)}) copy-start(f32[1024]{0:T(1024)S(1)} %get-tuple-element.33) | copy-start | bytes 12292
  95.4 4.6 %copy-start.17 = (f32[1024]{0:T(1024)}, f32[1024]{0:T(1024)S(1)}, u32[]{:S(2)}) copy-start(f32[1024]{0:T(1024)S(1)} %get-tuple-element.28) | copy-start | bytes 12292
  97.2 2.7 copy-start.8
  97.2 3.4 copy-start.3
  99.9 0.6 copy-start.23
  100.0 0.7 copy-start.6
  100.0 12.9 %copy-start.20 = (f32[512]{0:T(512)}, f32[512]{0:T(512)S(1)}, u32[]{:S(2)}) copy-start(f32[512]{0:T(512)S(1)} %get-tuple-element.32) | copy-start | bytes 6148
  121.2 5.8 %copy-start.22 = (f32[512]{0:T(512)S(1)}, f32[512]{0:T(512)}, u32[]{:S(2)}) copy-start(f32[512]{0:T(512)} %get-tuple-element.23) | copy-start | bytes 6148
  142.3 10.8 %slice-start = ((s8[8388608]{0:T(1024)(128)(4,1)}), s8[4194304]{0:T(1024)(128)(4,1)S(1)}, s32[]{:S(2)}) async-start(s8[8388608]{0:T(1024)(128)(4,1)} %bitcast.28), calls=%async_computation.8 | async-start | bytes 8388608
  144.6 3.8 %copy-start.25 = (f32[1024]{0:T(1024)}, f32[1024]{0:T(1024)S(1)}, u32[]{:S(2)}) copy-start(f32[1024]{0:T(1024)S(1)} %multiply_multiply_fusion) | copy-start | bytes 12292
  144.6 8.5 %slice-start.1 = ((s8[8388608]{0:T(1024)(128)(4,1)}), s8[4194304]{0:T(1024)(128)(4,1)S(1)}, s32[]{:S(2)}) async-start(s8[8388608]{0:T(1024)(128)(4,1)} %bitcast.28), calls=%async_computation.9 | async-start | bytes 8388608
  148.4 2.1 copy-start.13
  150.5 2.6 copy-start.2
  150.5 2.6 copy-start.7
  153.1 1.6 copy-start.24
  153.1 1.6 copy-start.9
  153.1 1.6 copy-start.21
  154.8 2.6 copy-start.27
  157.4 1.6 copy-start.11
  160.0 13.7 %copy-start.18 = (f32[1024]{0:T(1024)S(1)}, f32[1024]{0:T(1024)}, u32[]{:S(2)}) copy-start(f32[1024]{0:T(1024)} %copy-done.17) | copy-start | bytes 12292
  160.0 13.7 %copy-start.26 = (f32[1024]{0:T(1024)S(1)}, f32[1024]{0:T(1024)}, u32[]{:S(2)}) copy-start(f32[1024]{0:T(1024)} %copy-done.25) | copy-start | bytes 12292
  170.2 10.4 %all-to-all-start.4 = ((bf16[4,8,72,128]{3,2,1,0:T(8,128)(2,1)}), bf16[4,8,72,128]{3,2,1,0:T(8,128)(2,1)S(1)}, u32[]{:S(2)}, u32[]{:S(2)}) async-start(bf16[4,8,72,128]{3,2,1,0:T(8,128)(2,1)} %bitcast.33), calls=%async_computation.4 | async-start | bytes 1179648 | tf_op jit(solution)/shard_map/all_to_all | solution.py:97
  181.5 148.2 %all-to-all-start.5 = ((bf16[4,8,72,128]{3,2,0,1:T(8,128)(2,1)}), bf16[4,8,72,128]{3,2,0,1:T(8,128)(2,1)S(1)}, u32[]{:S(2)}, u32[]{:S(2)}) async-start(bf16[4,8,72,128]{3,2,0,1:T(8,128)(2,1)} %copy.29), calls=%async_computation.5 | async-start | bytes 1179648 | tf_op jit(solution)/shard_map/all_to_all | solution.py:96
  186.1 139.9 %all-reduce.3.cloned.1.call-start = ((), (), s32[]{:S(2)}) async-start(), calls=%async_computation.7 | async-start | bytes 2097152 | tf_op jit(solution)/shard_map/psum | solution.py:117
  345.6 3.5 copy-start.15
  345.6 4.1 %copy-start.1 = (f32[8192,128]{1,0:T(8,128)S(1)}, f32[8192,128]{1,0:T(8,128)}, u32[]{:S(2)}) copy-start(f32[8192,128]{1,0:T(8,128)} %param.10) | copy-start | bytes 12582916
Sparse Core Ops, SparseCore 0:
  96.4 24.8 all-gather.2
  193.0 132.9 all-reduce.2
where the time goes:
time: 363 us; the launch traced here: 362 us
  waiting for transfers between devices  135 us (37%)
  blocking collectives  99.8 us (27%)
  other arithmetic  45.6 us (13%)
  matrix products  41 us (11%)
  between operations  16.3 us (4%)
  local copies, waits for them, and re-layouts  12.4 us (3%)
  starting transfers between devices  11.7 us (3%)
    psum x1, waiting for transfers between devices, per_device(): lax.psum((user_first_g, user_second_g, item_first_g, item_second_g, loss_...  96.8 us
    psum x1, blocking collectives, per_device(): lax.psum((user_first_g, user_second_g, item_first_g, item_second_g, loss_...  40.8 us
    all_to_all x1, waiting for transfers between devices, per_device(): lax.all_to_all(lax.all_to_all(fetched, 'dp', split_axis=0, concat_axis=0,...  29.1 us
    dot_general x6, matrix products, tower_pass(): jnp.dot(hidden_act, second_w, precision=highest, preferred_element_type=j...  19.6 us
    all_to_all x1, blocking collectives, per_device(): lax.all_to_all(fetched, 'dp', split_axis=0, concat_axis=0, tiled=True)  18.2 us
    scatter-add x1, other arithmetic, per_device(): grad_rows = jnp.zeros_like(id_table).at[asked_rows.reshape(-1)].add(sent_...  15.8 us
    all_gather x1, blocking collectives, per_device(): lax.all_gather(user_vec, 'dp', axis=0, tiled=True).astype(jnp.bfloat16)  11.5 us
    all_to_all x1, blocking collectives, per_device(): lax.all_to_all(lax.all_to_all(fetch_rows[0], 'dp', split_axis=0, concat_a...  10.3 us
  transfers between devices with their start and end apart: 5, of which 4 were waited for; matrix products, arithmetic and copies ran while one was open for 4% of the time, Pallas kernels for 0%

commit v1 on v0

--- a/solution.py
+++ b/solution.py
@@ -2,6 +2,7 @@
 import jax.numpy as jnp
 from jax import lax
 from jax.sharding import PartitionSpec as P
+from jax.lax import psum
 
 EXAMPLES_ON_CHIP = 512
 highest = lax.Precision.HIGHEST
@@ -114,9 +115,9 @@
     new_state = ada_state + jnp.mean(grad_rows * grad_rows, axis=1)
     new_table = id_table - learn_rate * grad_rows / (jnp.sqrt(new_state)[:, None] + epsilon)
     loss_part = jnp.sum(log_z - matching_pair_logit)
-    summed = lax.psum(
-        (user_first_g, user_second_g, item_first_g, item_second_g, loss_part), ("dp", "shard")
-    )
+    summed = (user_first_g, user_second_g, item_first_g, item_second_g, loss_part)
+    for src_i in ("shard", "dp"):
+        summed = psum(summed, src_i)
     shard_number = lax.axis_size("dp") * lax.axis_size("shard")
     return (
         new_table,

time: 363 us -> 314 us (0.87)
  waiting for transfers between devices: 135 us -> 105 us
  blocking collectives: 99.8 us -> 85.5 us
    psum x1 -> x2, waiting for transfers between devices: 96.8 us -> 62.4 us  [per_device(): summed = psum(summed, src_i)]
    psum x1 -> x2, blocking collectives: 40.8 us -> 27.6 us  [per_device(): summed = psum(summed, src_i)]
  transfers between devices with their start and end apart: 5 -> 6, of which waited for: 4 -> 5; matrix products, arithmetic and copies ran while one was open for 4% -> 13% of each run, Pallas kernels for 0% -> 0%
where the time goes in v1:
time: 314 us; the launch traced here: 313 us
  waiting for transfers between devices  105 us (33%)
  blocking collectives  85.5 us (27%)
  other arithmetic  43 us (14%)
  matrix products  37.5 us (12%)
  between operations  16 us (5%)
  local copies, waits for them, and re-layouts  13.7 us (4%)
  starting transfers between devices  12.7 us (4%)
    psum x2, waiting for transfers between devices, per_device(): summed = psum(summed, src_i)  62.4 us
    all_to_all x1, waiting for transfers between devices, per_device(): lax.all_to_all(lax.all_to_all(fetched, 'dp', split_axis=0, concat_axis=0,...  29.1 us
    psum x2, blocking collectives, per_device(): summed = psum(summed, src_i)  27.6 us
    dot_general x6, matrix products, tower_pass(): jnp.dot(hidden_act, second_w, precision=highest, preferred_element_type=j...  19.7 us
    all_to_all x1, blocking collectives, per_device(): lax.all_to_all(fetched, 'dp', split_axis=0, concat_axis=0, tiled=True)  18.2 us
    scatter-add x1, other arithmetic, per_device(): grad_rows = jnp.zeros_like(id_table).at[asked_rows.reshape(-1)].add(sent_...  15.7 us
    all_gather x1, waiting for transfers between devices, per_device(): lax.all_gather(item_bf, 'dp', axis=0, tiled=True)  11.3 us
    all_gather x1, blocking collectives, per_device(): lax.all_gather(user_vec, 'dp', axis=0, tiled=True).astype(jnp.bfloat16)  11.1 us
  transfers between devices with their start and end apart: 6, of which 5 were waited for; matrix products, arithmetic and copies ran while one was open for 13% of the time, Pallas kernels for 0%

profile of v1, /device:TPU:0, one launch (start us, length us, event | category | flops | bytes accessed | tf_op | source)
XLA Modules:
  0.0 313.3 jit_solution(8629353732001511194)
XLA Ops:
  7.2 0.0 copy-start
  7.2 10.0 %all_to_all.30 = s32[4,8,72]{2,1,0:T(8,128)S(1)} all-to-all(s32[4,8,72]{2,1,0:T(8,128)} %bitcast.32), channel_id=1, replica_groups=mesh['dp'=4,'shard'=8] {'dp'}, dimensions={0} | all-to-all | bytes 18432 | tf_op jit(solution)/shard_map/all_to_all | solution.py:50
  17.2 10.3 %all_to_all.31 = s32[4,8,72]{2,0,1:T(4,128)S(1)} all-to-all(s32[4,8,72]{2,0,1:T(4,128)S(1)} %copy.24), channel_id=1, replica_groups=mesh['dp'=4,'shard'=8] {'shard'}, dimensions={1} | all-to-all | bytes 18432 | tf_op jit(solution)/shard_map/all_to_all | solution.py:49
  27.6 0.1 reshape.171
  27.7 6.1 %gather_fusion = f32[2304,128]{1,0:T(8,128)S(1)} fusion(f32[8192,128]{1,0:T(8,128)} %param.10, s32[3072]{0:T(1024)S(1)} %pad_clamp_fusion), kind=kCustom, calls=%fused_computation | custom fusion | bytes 2368512 | tf_op jit(solution)/shard_map/jit(_take)/gather | solution.py:56
  33.8 0.5 broadcast_select_fusion
  34.3 18.2 %all_to_all.32 = f32[4,8,72,128]{3,2,1,0:T(8,128)S(1)} all-to-all(f32[4,8,72,128]{3,2,1,0:T(8,128)S(1)} %broadcast_select_fusion), channel_id=1, replica_groups=mesh['dp'=4,'shard'=8] {'dp'}, dimensions={0} | all-to-all | bytes 2359296 | tf_op jit(solution)/shard_map/all_to_all | solution.py:60
  52.5 1.1 copy.27
  53.6 3.6 %all-to-all-start.3 = ((f32[4,8,72,128]{3,2,0,1:T(8,128)}), f32[4,8,72,128]{3,2,0,1:T(8,128)S(1)}, u32[]{:S(2)}, u32[]{:S(2)}) async-start(f32[4,8,72,128]{3,2,0,1:T(8,128)} %copy.27), calls=%async_computation.3 | async-start | bytes 2359296 | tf_op jit(solution)/shard_map/all_to_all | solution.py:59
  57.2 0.0 all-gather.3.cloned.1.call-start
  57.4 29.1 %all-to-all-done.3 = f32[4,8,72,128]{3,2,0,1:T(8,128)S(1)} async-done(((f32[4,8,72,128]{3,2,0,1:T(8,128)}), f32[4,8,72,128]{3,2,0,1:T(8,128)S(1)}, u32[]{:S(2)}, u32[]{:S(2)}) %all-to-all-start.3) | async-done | bytes 1179680 | tf_op jit(solution)/shard_map/all_to_all | solution.py:59
  86.5 0.1 copy.28
  86.6 0.0 copy-start.15
  86.6 2.6 gather_fusion.1
  89.2 0.3 broadcast_select_fusion.1
  89.5 1.8 fusion.30
  91.3 0.0 copy-start.6
  91.3 0.0 copy-start.13
  91.3 2.7 multiply_reduce_fusion.2
  94.1 0.9 divide_convert_fusion
  95.0 0.0 all-gather.3.cloned.1.call-update
  95.0 1.0 fusion.41
  96.0 0.0 copy-start.5
  96.0 2.6 multiply_reduce_fusion.4
  98.7 0.1 fusion.38
  98.8 11.1 %all_gather.10 = bf16[2048,128]{0,1:T(8,128)(2,1)S(1)} all-gather(bf16[512,128]{0,1:T(8,128)(2,1)S(1)} %get-tuple-element.28), channel_id=1, replica_groups=mesh['dp'=4,'shard'=8] {'dp'}, dimensions={0}, use_global_device_ids=true | all-gather | bytes 655360 | tf_op jit(solution)/shard_map/all_gather | solution.py:83
  109.9 11.3 %all-gather.3.cloned.1.call-done = bf16[4096,128]{0,1:T(8,128)(2,1)} async-done(((bf16[1024,128]{0,1:T(8,128)(2,1)}), bf16[4096,128]{0,1:T(8,128)(2,1)}) %all-gather.3.cloned.1.call-update) | async-done | bytes 1048592 | tf_op jit(solution)/shard_map/all_gather | solution.py:79
  121.2 2.8 fusion
  124.0 0.6 subtract_reduce_fusion
  124.6 2.3 multiply_reduce_fusion.3
  126.9 8.2 %all-gather = f32[4,1,512]{2,1,0:T(1,128)S(1)} all-gather(f32[1,1,512]{2,1,0:T(1,128)S(1)} %bitcast.34), channel_id=1, replica_groups=mesh['dp'=4,'shard'=8] {'dp'}, dimensions={0}, use_global_device_ids=true | all-gather | bytes 10240 | tf_op jit(solution)/shard_map/all_gather | solution.py:84
  135.1 2.1 fusion.10
  137.3 0.1 fusion.37
  137.3 0.1 multiply_reduce_fusion.1
  137.4 0.7 copy-done.9
  138.1 4.4 %fusion.6 = f32[1024,512]{1,0:T(8,128)S(1)} fusion(f32[1024,512]{1,0:T(8,128)} %copy-done.6, f32[512,128]{1,0:T(8,128)S(1)} %copy-done, f32[1024,128]{0,1:T(8,128)} %copy-done.7, f32[1024,128]{0,1:T(8,128)} %copy-done.9, f32[1024]{0:T(1024)S(1)} %multiply_multiply_fusion, f32[1024]{0:T(1024)S(1)} %get-tuple-element.32), kind=kOutput, calls=%fused_computation.14 | convolution fusion | flops 810680320 | bytes 5513216 | tf_op jit(solution)/shard_map/transpose(jvp())/dot_general | solution.py:18
  142.5 2.6 fusion.58
  145.2 1.3 fusion.19
  146.5 1.0 copy-done.2
  147.4 1.7 fusion.57
  149.1 10.4 %scatter_custom_fusion = f32[2304,128]{1,0:T(8,128)} fusion(s32[1536]{0:T(1024)S(1)} %fusion.48, f32[1024,128]{1,0:T(8,128)} %fusion.58, f32[]{:T(128)} %constant.111, f32[512,128]{1,0:T(8,128)} %fusion.57, f32[]{:T(128)} %constant.90.clone.1), kind=kCustom, calls=%fused_computation.28 | custom fusion | flops 393216 | bytes 1966088 | tf_op jit(solution)/shard_map/scatter-add | solution.py:96
  159.5 2.2 convert_element_type.35
  161.6 4.4 %all-to-all-start.4 = ((bf16[4,8,72,128]{3,2,1,0:T(8,128)(2,1)}), bf16[4,8,72,128]{3,2,1,0:T(8,128)(2,1)}, u32[]{:S(2)}, u32[]{:S(2)}) async-start(bf16[4,8,72,128]{3,2,1,0:T(8,128)(2,1)} %bitcast.31), calls=%async_computation.4 | async-start | bytes 1179648 | tf_op jit(solution)/shard_map/all_to_all | solution.py:98
  166.0 2.1 fusion.28
  168.1 2.6 fusion.43
  170.8 2.1 all-to-all-done.4
  172.8 1.9 copy.29
  174.7 4.6 %all-to-all-start.5 = ((bf16[4,8,72,128]{3,2,0,1:T(8,128)(2,1)}), bf16[4,8,72,128]{3,2,0,1:T(8,128)(2,1)S(1)}, u32[]{:S(2)}, u32[]{:S(2)}) async-start(bf16[4,8,72,128]{3,2,0,1:T(8,128)(2,1)} %copy.29), calls=%async_computation.5 | async-start | bytes 1179648 | tf_op jit(solution)/shard_map/all_to_all | solution.py:97
  179.4 0.0 all-reduce.5.cloned.1.call-start
  179.4 1.5 fusion.39
  180.9 6.0 %fusion.32 = f32[512,128]{1,0:T(8,128)} fusion(f32[1024,512]{1,0:T(8,128)} %copy-done.6, f32[1024,128]{0,1:T(8,128)S(1)} %copy-done.8, f32[1024,128]{0,1:T(8,128)} %copy-done.9, f32[1024]{0:T(1024)S(1)} %multiply_multiply_fusion, f32[1024]{0:T(1024)S(1)} %get-tuple-element.32), kind=kOutput, calls=%fused_computation.45 | convolution fusion | flops 808058880 | bytes 3416064 | tf_op jit(solution)/shard_map/transpose(jvp())/dot_general | solution.py:18
  186.9 0.0 all-reduce.5.cloned.1.call-update
  187.0 0.0 all-reduce.7.cloned.1.call-start
  187.0 17.9 %psum.78 = f32[]{:T(128)} all-reduce(f32[]{:T(128)} %get-tuple-element.33), channel_id=1, replica_groups=mesh['dp'=4,'shard'=8] {'shard'}, use_global_device_ids=true, to_apply=%region_18.19 | all-reduce | flops 1 | bytes 8 | tf_op jit(solution)/shard_map/psum | solution.py:120
  205.0 9.7 %psum.79 = f32[]{:T(128)} all-reduce(f32[]{:T(128)} %psum.78), channel_id=1, replica_groups=mesh['dp'=4,'shard'=8] {'dp'}, use_global_device_ids=true, to_apply=%region_19.20 | all-reduce | flops 1 | bytes 8 | tf_op jit(solution)/shard_map/psum | solution.py:120
  215.3 31.7 %all-reduce.5.cloned.1.call-done = (f32[128,512]{1,0:T(8,128)}, f32[512,128]{1,0:T(8,128)}, f32[128,512]{1,0:T(8,128)}, f32[512,128]{1,0:T(8,128)}) async-done(((f32[128,512]{1,0:T(8,128)}, f32[512,128]{1,0:T(8,128)}, f32[128,512]{1,0:T(8,128)}, f32[512,128]{1,0:T(8,128)}), (f32[128,512]{1,0:T(8,128)}, f32[512,128]{1,0:T(8,128)}, f32[128,512]{1,0:T(8,128)}, ...) | async-done | bytes 1048592 | tf_op jit(solution)/shard_map/psum | solution.py:120
  247.0 0.0 all-reduce.7.cloned.1.call-update
  247.1 15.7 %scatter_custom_fusion.1 = f32[8192,128]{1,0:T(8,128)} fusion(s32[2304]{0:T(1024)S(1)} %fusion.47, f32[]{:T(128)} %constant.90.clone.1, bf16[2304,128]{1,0:T(8,128)(2,1)S(1)} %bitcast.30), kind=kCustom, calls=%fused_computation.17 | custom fusion | flops 589824 | bytes 4784132 | tf_op jit(solution)/shard_map/scatter-add | solution.py:113
  262.8 3.5 %multiply_reduce_fusion = f32[8192]{0:T(1024)S(1)} fusion(f32[8192,128]{1,0:T(8,128)} %scatter_custom_fusion.1), kind=kLoop, calls=%fused_computation.10 | loop fusion | flops 2088960 | bytes 4227072 | tf_op jit(solution)/shard_map/reduce_sum | solution.py:115
  266.3 0.6 sqrt_add_fusion
  267.0 4.3 %divide_subtract_fusion = f32[8192,128]{1,0:T(8,128)} fusion(f32[8192,128]{1,0:T(8,128)S(1)} %copy-done.1, f32[8192,128]{1,0:T(8,128)} %scatter_custom_fusion.1, f32[8192]{0:T(1024)S(1)} %get-tuple-element.29), kind=kLoop, calls=%fused_computation.9 | loop fusion | flops 3145728 | bytes 12615680 | tf_op jit(solution)/shard_map/sub | solution.py:116
  271.3 30.7 %all-reduce.7.cloned.1.call-done = (f32[128,512]{1,0:T(8,128)}, f32[512,128]{1,0:T(8,128)}, f32[128,512]{1,0:T(8,128)}, f32[512,128]{1,0:T(8,128)}) async-done(((f32[128,512]{1,0:T(8,128)}, f32[512,128]{1,0:T(8,128)}, f32[128,512]{1,0:T(8,128)}, f32[512,128]{1,0:T(8,128)}), (f32[128,512]{1,0:T(8,128)}, f32[512,128]{1,0:T(8,128)}, f32[128,512]{1,0:T(8,128)}, ...) | async-done | bytes 1048592 | tf_op jit(solution)/shard_map/psum | solution.py:120
  301.9 1.9 broadcast_multiply_fusion.2
  303.8 1.9 broadcast_multiply_fusion
  (53 shorter events, 0.3 us)
Async XLA Ops:
  7.2 84.1 %copy-start = (f32[512,128]{1,0:T(8,128)S(1)}, f32[512,128]{1,0:T(8,128)}, u32[]{:S(2)}) copy-start(f32[512,128]{1,0:T(8,128)} %param.15) | copy-start | bytes 786436
  52.5 4.7 %copy-start.20 = (s32[1,1536]{1,0:T(1,128)S(1)}, s32[1,1536]{1,0:T(1,128)}, u32[]{:S(2)}) copy-start(s32[1,1536]{1,0:T(1,128)} %param.17) | copy-start | bytes 18436
  53.6 32.9 %all-to-all-start.3 = ((f32[4,8,72,128]{3,2,0,1:T(8,128)}), f32[4,8,72,128]{3,2,0,1:T(8,128)S(1)}, u32[]{:S(2)}, u32[]{:S(2)}) async-start(f32[4,8,72,128]{3,2,0,1:T(8,128)} %copy.27), calls=%async_computation.3 | async-start | bytes 2359296 | tf_op jit(solution)/shard_map/all_to_all | solution.py:59
  57.2 64.0 %all-gather.3.cloned.1.call-start = ((), (), s32[]{:S(2)}) async-start(), calls=%async_computation.6 | async-start | bytes 1310720 | tf_op jit(solution)/shard_map/all_gather | solution.py:79
  86.6 2.9 copy-start.15
  91.3 2.8 copy-start.6
  91.3 3.7 %copy-start.13 = (f32[128,512]{1,0:T(8,128)S(1)}, f32[128,512]{1,0:T(8,128)}, u32[]{:S(2)}) copy-start(f32[128,512]{1,0:T(8,128)} %param.12) | copy-start | bytes 786436
  94.1 43.3 %copy-start.7 = (f32[1024,128]{0,1:T(8,128)}, f32[1024,128]{0,1:T(8,128)S(1)}, u32[]{:S(2)}) copy-start(f32[1024,128]{0,1:T(8,128)S(1)} %get-tuple-element.38) | copy-start | bytes 1572868
  96.0 2.7 copy-start.10
  96.0 2.7 copy-start.5
  121.2 3.4 %copy-start.4 = (bf16[4096,128]{0,1:T(8,128)(2,1)S(1)}, bf16[4096,128]{0,1:T(8,128)(2,1)}, u32[]{:S(2)}) copy-start(bf16[4096,128]{0,1:T(8,128)(2,1)} %all-gather.3.cloned.1.call-done) | copy-start | bytes 3145732
  137.3 0.8 copy-start.9
  138.1 4.4 %copy-start.16 = (f32[128,512]{1,0:T(8,128)S(1)}, f32[128,512]{1,0:T(8,128)}, u32[]{:S(2)}) copy-start(f32[128,512]{1,0:T(8,128)} %param.14) | copy-start | bytes 786436
  142.5 2.6 copy-start.11
  142.5 2.6 copy-start.17
  142.5 2.6 copy-start.21
  145.1 2.3 copy-start.14
  146.5 1.0 copy-start.2
  161.6 11.2 %all-to-all-start.4 = ((bf16[4,8,72,128]{3,2,1,0:T(8,128)(2,1)}), bf16[4,8,72,128]{3,2,1,0:T(8,128)(2,1)}, u32[]{:S(2)}, u32[]{:S(2)}) async-start(bf16[4,8,72,128]{3,2,1,0:T(8,128)(2,1)} %bitcast.31), calls=%async_computation.4 | async-start | bytes 1179648 | tf_op jit(solution)/shard_map/all_to_all | solution.py:98
  166.0 2.1 copy-start.12
  166.0 2.1 copy-start.18
  170.8 8.7 %copy-start.3 = (f32[512,512]{1,0:T(8,128)S(1)}, f32[512,512]{1,0:T(8,128)}, u32[]{:S(2)}) copy-start(f32[512,512]{1,0:T(8,128)} %copy-done.2) | copy-start | bytes 3145732
  170.8 10.1 %copy-start.8 = (f32[1024,128]{0,1:T(8,128)S(1)}, f32[1024,128]{0,1:T(8,128)}, u32[]{:S(2)}) copy-start(f32[1024,128]{0,1:T(8,128)} %copy-done.7) | copy-start | bytes 1572868
  174.7 72.3 %all-to-all-start.5 = ((bf16[4,8,72,128]{3,2,0,1:T(8,128)(2,1)}), bf16[4,8,72,128]{3,2,0,1:T(8,128)(2,1)S(1)}, u32[]{:S(2)}, u32[]{:S(2)}) async-start(bf16[4,8,72,128]{3,2,0,1:T(8,128)(2,1)} %copy.29), calls=%async_computation.5 | async-start | bytes 1179648 | tf_op jit(solution)/shard_map/all_to_all | solution.py:97
  179.4 67.6 %all-reduce.5.cloned.1.call-start = ((), (), s32[]{:S(2)}) async-start(), calls=%async_computation.7 | async-start | bytes 2097152 | tf_op jit(solution)/shard_map/psum | solution.py:120
  187.0 115.0 %all-reduce.7.cloned.1.call-start = ((), (), s32[]{:S(2)}) async-start(), calls=%async_computation.8 | async-start | bytes 2097152 | tf_op jit(solution)/shard_map/psum | solution.py:120
  262.8 3.5 %copy-start.19 = (f32[8192]{0:T(1024)S(1)}, f32[8192]{0:T(1024)}, u32[]{:S(2)}) copy-start(f32[8192]{0:T(1024)} %param.11) | copy-start | bytes 98308
  262.8 4.2 %copy-start.1 = (f32[8192,128]{1,0:T(8,128)S(1)}, f32[8192,128]{1,0:T(8,128)}, u32[]{:S(2)}) copy-start(f32[8192,128]{1,0:T(8,128)} %param.10) | copy-start | bytes 12582916
Sparse Core Ops, SparseCore 0:
  95.1 26.0 all-gather.2
  187.1 59.8 all-reduce.4
  250.2 51.6 all-reduce.6
